TPU v7x, 512 devices: a whole 4x4x16 slice. The times are simulated.
512 devices in a mesh: dp: 64 (over z, y), owner: 8 (over x, core).
Axes of the slice: x: 4, y: 4, z: 16, core: 2. Of those that a mesh axis runs over, the one named last changes fastest.
Arguments:
- query_out: bfloat16 [512, 16384], P('dp', 'owner'), may hold values from -6 to 6
- query_in: bfloat16 [512, 8192], P('dp'), may hold values from -6 to 6
- train_out: bfloat16 [512, 16384], P('dp', 'owner'), may hold values from -6 to 6
- train_in: bfloat16 [512, 8192], P('dp'), may hold values from -6 to 6
- basis_out: bfloat16 [96, 256, 256], P('owner'), may hold values from -1 to 1, as said below
- basis_in: bfloat16 [64, 128, 128], P('dp'), may hold values from -1 to 1, as said below
- eigvals: float32 [24576, 8192], P('owner', 'dp'), may hold values from 0.1 to 10
- owner_map: int32 [64], replicated, may hold values from 0 to 7, as said below
Outputs:
- scores: float32 [8, 32], replicated
Inputs may be any that keep to these rules, and one draw needn't show every extreme that they name: owner_map[b] is the owner of hidden block b. Blocks form ranges of 8 in order; a block of range r is owned by r or by r xor 1. Of two such partner owners one holds exactly 12 blocks and keeps 12 // 2 of its own range, the other holds 4 blocks and keeps 8 - 12 // 2 of its own range. `basis_out`: each [256, 256] block is an orthogonal matrix rounded to bfloat16; block o * 12 + s belongs to the s-th block, in block order, that owner o holds; blocks past an owner's count are not read. `basis_in`: each [128, 128] block is an orthogonal matrix rounded to bfloat16.
All inputs are finite; a program needn't handle non-finite values.
Results may differ from a plain program's by a relative error of at most 0.0067.
Values may be sent and summed in bfloat16 or wider, within the bound.
No kernel may reach another device: no remote copies, remote signals or barrier semaphores. Data moves between devices by JAX's collectives and lax.ppermute only.
A program may use at most 64 MiB of HBM per device.

v0:
```python
import math

import jax
import jax.numpy as jnp
from jax import lax
from jax.sharding import PartitionSpec as P

NQ = 8
ET = 16


DAMPING = 0.1


def from_partner(array, axis, stride):
    return lax.ppermute(array, axis, [(i, i ^ 1 << stride) for i in range(lax.axis_size(axis))])


def slot_tables(owner_map, owner_index, blocks_own, capacity):
    pair_count = 2 * blocks_own
    pair_base = owner_index // 2 * pair_count
    pair_owner = lax.dynamic_slice_in_dim(owner_map, pair_base, pair_count)
    owned_mask = (pair_owner == owner_index).astype(jnp.int32)
    slot_rank = jnp.cumsum(owned_mask) - 1
    slot_ids = jnp.arange(capacity, dtype=jnp.int32)
    pair_hot = (owned_mask[:, None] == 1) & (slot_rank[:, None] == slot_ids[None, :])
    own_start = owner_index % 2 * blocks_own
    other_start = blocks_own - own_start
    keep_hot = lax.dynamic_slice_in_dim(pair_hot, own_start, blocks_own, 0)
    other_hot = lax.dynamic_slice_in_dim(pair_hot, other_start, blocks_own, 0)
    send_ids = jnp.arange(capacity // 2, dtype=jnp.int32)
    from_other = lax.dynamic_slice_in_dim(owned_mask, other_start, blocks_own)
    other_rank = jnp.cumsum(from_other) - 1
    arrive_hot = (from_other[:, None] == 1) & (other_rank[:, None] == send_ids[None, :])
    arrive_slot = jnp.dot(arrive_hot.T.astype(jnp.float32), other_hot.astype(jnp.float32))
    to_other = 1 - lax.dynamic_slice_in_dim(owned_mask, own_start, blocks_own)
    depart_rank = jnp.cumsum(to_other) - 1
    depart_hot = (to_other[:, None] == 1) & (depart_rank[:, None] == send_ids[None, :])
    return (
        keep_hot.astype(jnp.bfloat16),
        depart_hot.astype(jnp.bfloat16),
        arrive_slot.astype(jnp.bfloat16),
    )


def departing(tokens, depart_hot, block_width):
    blocks = tokens.reshape(tokens.shape[0], -1, block_width)
    return jnp.einsum("rpk,ps->rsk", blocks, depart_hot, preferred_element_type=jnp.float32).astype(
        jnp.bfloat16
    )


def to_slots(tokens, arrived, keep_hot, arrive_slot, block_width):
    blocks = tokens.reshape(tokens.shape[0], -1, block_width)
    kept_part = jnp.einsum("rpk,pc->rck", blocks, keep_hot, preferred_element_type=jnp.float32)
    moved_part = jnp.einsum("rsk,sc->rck", arrived, arrive_slot, preferred_element_type=jnp.float32)
    return (kept_part + moved_part).astype(jnp.bfloat16)


def rotate_outputs(slotted, basis_out):
    return jnp.einsum(
        "rck,ckl->rcl", slotted, basis_out, preferred_element_type=jnp.float32
    ).astype(jnp.bfloat16)


def rotate_inputs(columns_local, basis_in):
    token_count = columns_local.shape[0]
    blocks = columns_local.reshape(token_count, basis_in.shape[0], basis_in.shape[1])
    turned = jnp.einsum("tnb,nbc->tnc", blocks, basis_in, preferred_element_type=jnp.float32)
    return turned.astype(jnp.bfloat16).reshape(token_count, -1)


def condition(query_rot, query_act, eigvals, basis_in, basis_out):
    capacity, block_width = (basis_out.shape[0], basis_out.shape[1])
    in_blocks, in_width = (basis_in.shape[0], basis_in.shape[1])
    per_query = query_rot.shape[0] // NQ
    query_flat = query_rot.reshape(query_rot.shape[0], capacity * block_width)
    shifted = eigvals + DAMPING
    results = []
    for query_index in range(NQ):
        left_side = query_flat[query_index * per_query : (query_index + 1) * per_query]
        right_side = query_act[query_index * per_query : (query_index + 1) * per_query]
        moment = lax.dot_general(
            left_side, right_side, (((0,), (0,)), ((), ())), preferred_element_type=jnp.float32
        )
        damped = (moment / shifted).astype(jnp.bfloat16)
        half_back = jnp.einsum(
            "fnb,ncb->fnc",
            damped.reshape(-1, in_blocks, in_width),
            basis_in,
            preferred_element_type=jnp.float32,
        ).astype(jnp.bfloat16)
        restored = jnp.einsum(
            "ckl,cld->ckd",
            basis_out,
            half_back.reshape(capacity, block_width, -1),
            preferred_element_type=jnp.float32,
        ).astype(jnp.bfloat16)
        results.append(restored.reshape(capacity * block_width, -1))
    return jnp.stack(results)


def score_tokens(precond, train_slots, train_inputs, example_count):
    projected = jnp.einsum("tf,qfd->qtd", train_slots, precond, preferred_element_type=jnp.float32)
    per_token = jnp.sum(projected * train_inputs.astype(jnp.float32)[None], axis=2)
    token_ids = jnp.arange(train_slots.shape[0], dtype=jnp.int32)
    example_hot = (
        token_ids[:, None] // ET == jnp.arange(example_count, dtype=jnp.int32)[None, :]
    ).astype(jnp.float32)
    return jnp.dot(per_token, example_hot, precision=lax.Precision.HIGHEST)


def local(query_out, query_in, train_out, train_in, basis_out, basis_in, eigvals, owner_map):
    owner_index = lax.axis_index("owner")
    capacity = basis_out.shape[0]
    block_width = basis_out.shape[1]
    blocks_own = query_out.shape[1] // block_width
    query_local = query_out.shape[0]
    keep_hot, depart_hot, arrive_slot = slot_tables(owner_map, owner_index, blocks_own, capacity)
    query_cols, train_cols = (
        lax.all_to_all(query_in, "dp", split_axis=1, concat_axis=0, tiled=True),
        lax.all_to_all(train_in, "dp", split_axis=1, concat_axis=0, tiled=True),
    )
    query_act = rotate_inputs(query_cols, basis_in)
    example_count = train_cols.shape[0] // ET
    local_tokens = jnp.concatenate([query_out, train_out], 0)
    leaving = departing(local_tokens, depart_hot, block_width)
    arrived = from_partner(leaving, "owner", 0)
    slotted = to_slots(local_tokens, arrived, keep_hot, arrive_slot, block_width)
    query_rot = rotate_outputs(slotted[:query_local], basis_out)
    train_local = slotted[query_local:]
    query_all = lax.all_gather(query_rot, "dp", axis=0, tiled=True)
    precond = condition(query_all, query_act, eigvals, basis_in, basis_out)
    piece_slots = lax.all_gather(train_local, "dp", axis=0, tiled=True)
    row_count = piece_slots.shape[0]
    partial_scores = score_tokens(
        precond, piece_slots.reshape(row_count, -1), train_cols, example_count
    )
    scores = lax.psum(partial_scores, ("dp", "owner"))
    per_query = query_act.shape[0] // NQ
    hidden_total = query_out.shape[1] * lax.axis_size("owner")
    score_scale = 1.0 / math.sqrt(per_query * ET * hidden_total * query_in.shape[1])
    return scores * score_scale


def solution(mesh):
    in_specs = (
        P("dp", "owner"),
        P("dp", None),
        P("dp", "owner"),
        P("dp", None),
        P("owner", None, None),
        P("dp", None, None),
        P("owner", "dp"),
        P(),
    )
    out_specs = P()
    return jax.shard_map(local, mesh=mesh, in_specs=in_specs, out_specs=out_specs, check_vma=False)
```

profile of v0, /device:TPU:1, one launch (start us, length us, event | category | flops | bytes accessed | tf_op | source)
XLA Modules:
  0.0 418.7 jit_solution(11607726487385089527)
XLA Ops:
  8.7 8.7 %collective-permute-start = (bf16[16,6,256]{2,1,0:T(8,128)(2,1)S(1)}, bf16[16,6,256]{2,1,0:T(8,128)(2,1)S(1)}, u32[]{:S(2)}, u32[]{:S(2)}) collective-permute-start(bf16[16,6,256]{2,1,0:T(8,128)(2,1)S(1)} %fusion.20), channel_id=1, source_target_pairs={{0,1},{1,0},{2,3},{3,2},{4,5},{5,4},{6,7},{7,6},{8,9},{9,8},{10,11... | collective-permute-start | bytes 147464 | tf_op jit(solution)/shard_map/ppermute | solution.py:16
  19.8 28.1 %all_to_all.29 = bf16[8,64,128]{2,0,1:T(8,128)(2,1)S(1)} all-to-all(bf16[8,64,128]{2,0,1:T(8,128)(2,1)S(1)} %bitcast.263), channel_id=1, replica_groups=mesh['dp'=64,'owner'=8] {'dp'}, dimensions={1} | all-to-all | bytes 262144 | tf_op jit(solution)/shard_map/all_to_all | solution.py:122
  47.9 6.4 %all-to-all-start = ((bf16[8,64,128]{2,0,1:T(8,128)(2,1)}), bf16[8,64,128]{2,0,1:T(8,128)(2,1)S(1)}, u32[]{:S(2)}, u32[]{:S(2)}) async-start(bf16[8,64,128]{2,0,1:T(8,128)(2,1)} %bitcast.12), calls=%async_computation | async-start | bytes 262144 | tf_op jit(solution)/shard_map/all_to_all | solution.py:121
  56.1 12.7 %all-to-all-done = bf16[8,64,128]{2,0,1:T(8,128)(2,1)S(1)} async-done(((bf16[8,64,128]{2,0,1:T(8,128)(2,1)}), bf16[8,64,128]{2,0,1:T(8,128)(2,1)S(1)}, u32[]{:S(2)}, u32[]{:S(2)}) %all-to-all-start) | async-done | bytes 131104 | tf_op jit(solution)/shard_map/all_to_all | solution.py:121
  69.7 80.6 %all-gather.3.cloned.1.call-done = bf16[512,12,256]{2,0,1:T(8,128)(2,1)} async-done(((bf16[8,12,256]{2,0,1:T(8,128)(2,1)}), bf16[512,12,256]{2,0,1:T(8,128)(2,1)}) %all-gather.3.cloned.1.call-update) | async-done | bytes 3145744 | tf_op jit(solution)/shard_map/all_gather | solution.py:132
  150.3 3.3 slice_bitcast_fusion
  153.6 2.1 convolution_convert_fusion.7
  157.1 1.0 copy.135
  158.1 3.1 convolution_convert_fusion.6
  161.2 1.8 fusion.10
  163.0 1.2 copy.93
  164.1 1.4 copy.113
  165.6 1.8 copy.136
  167.3 3.2 convolution_convert_fusion.5
  170.5 2.7 fusion.11
  173.2 2.3 copy.96
  175.5 2.3 copy.114
  177.7 1.8 copy.137
  179.6 3.2 convolution_convert_fusion.4
  182.8 2.7 fusion.12
  185.4 2.3 copy.99
  187.7 2.3 copy.115
  190.1 1.8 copy.138
  191.8 3.2 convolution_convert_fusion.3
  195.0 2.7 fusion.13
  197.7 2.3 copy.102
  200.0 2.3 copy.116
  202.3 1.8 copy.139
  204.1 3.2 convolution_convert_fusion.2
  207.3 2.7 fusion.14
  210.0 2.3 copy.105
  212.3 2.3 copy.117
  214.6 1.8 copy.140
  216.4 3.2 convolution_convert_fusion.1
  219.5 2.9 fusion.15
  222.4 2.3 copy.108
  224.7 2.4 copy.118
  227.9 3.2 convolution_convert_fusion
  231.1 2.7 fusion.16
  233.8 2.3 copy.111
  236.1 2.3 copy.119
  238.3 0.9 constant_dynamic-update-slice_fusion.7
  240.2 0.9 constant_dynamic-update-slice_fusion.5
  244.0 1.0 constant_dynamic-update-slice_fusion.1
  245.9 42.4 %all-gather.5.cloned.1.call-done = bf16[512,12,256]{2,0,1:T(8,128)(2,1)} async-done(((bf16[8,12,256]{2,0,1:T(8,128)(2,1)}), bf16[512,12,256]{2,0,1:T(8,128)(2,1)}) %all-gather.5.cloned.1.call-update) | async-done | bytes 3145744 | tf_op jit(solution)/shard_map/all_gather | solution.py:134
  288.4 4.7 %copy.121 = bf16[512,12,256]{0,2,1:T(8,128)(2,1)} copy(bf16[512,12,256]{2,0,1:T(8,128)(2,1)} %all-gather.5.cloned.1.call-done) | data formatting | bytes 6291456 | tf_op jit(solution)/shard_map/all_gather | solution.py:134
  293.1 7.1 %fusion.8 = f32[8,512]{1,0:T(8,128)S(1)} fusion(bf16[8,3072,128]{1,2,0:T(8,128)(2,1)} %constant_dynamic-update-slice_fusion, bf16[512,3072,1]{0,1,2:T(8,128)(2,1)} %bitcast.235, f32[512,128]{0,1:T(8,128)S(1)} %copy-done.7), kind=kOutput, calls=%fused_computation.25 | convolution fusion | flops 3222269952 | bytes 9715712 | tf_op jit(solution)/shard_map/tf,qfd->qtd/dot_general | solution.py:104
  300.5 110.8 %psum.7 = f32[8,32]{1,0:T(8,128)S(1)} all-reduce(f32[8,32]{1,0:T(8,128)S(1)} %fusion.39), channel_id=1, replica_groups=mesh['dp'=64,'owner'=8] {'dp','owner'}, use_global_device_ids=true, to_apply=%region_4.5 | all-reduce | flops 256 | bytes 2048 | tf_op jit(solution)/shard_map/psum | solution.py:139
  (60 shorter events, 14.8 us)
Async XLA Ops:
  6.5 12.3 %copy-start = (bf16[12,256,256]{2,1,0:T(8,128)(2,1)S(1)}, bf16[12,256,256]{2,1,0:T(8,128)(2,1)}, u32[]{:S(2)}) copy-start(bf16[12,256,256]{2,1,0:T(8,128)(2,1)} %param.12) | copy-start | bytes 4718596
  6.5 143.8 %all-gather.3.cloned.1.call-start = ((), (), s32[]{:S(2)}) async-start(), calls=%async_computation.2 | async-start | bytes 3194880 | tf_op jit(solution)/shard_map/all_gather | solution.py:132
  8.5 11.3 %copy-start.8 = (bf16[8,8192]{1,0:T(8,128)(2,1)S(1)}, bf16[8,8192]{1,0:T(8,128)(2,1)}, u32[]{:S(2)}) copy-start(bf16[8,8192]{1,0:T(8,128)(2,1)} %param.11) | copy-start | bytes 393220
  8.7 9.6 %collective-permute-start = (bf16[16,6,256]{2,1,0:T(8,128)(2,1)S(1)}, bf16[16,6,256]{2,1,0:T(8,128)(2,1)S(1)}, u32[]{:S(2)}, u32[]{:S(2)}) collective-permute-start(bf16[16,6,256]{2,1,0:T(8,128)(2,1)S(1)} %fusion.20), channel_id=1, source_target_pairs={{0,1},{1,0},{2,3},{3,2},{4,5},{5,4},{6,7},{7,6},{8,9},{9,8},{10,11... | collective-permute-start | bytes 147464 | tf_op jit(solution)/shard_map/ppermute | solution.py:16
  18.8 50.0 %copy-start.9 = (bf16[1,128,128]{2,1,0:T(8,128)(2,1)S(1)}, bf16[1,128,128]{2,1,0:T(8,128)(2,1)}, u32[]{:S(2)}) copy-start(bf16[1,128,128]{2,1,0:T(8,128)(2,1)} %param.13) | copy-start | bytes 98308
  47.9 20.9 %all-to-all-start = ((bf16[8,64,128]{2,0,1:T(8,128)(2,1)}), bf16[8,64,128]{2,0,1:T(8,128)(2,1)S(1)}, u32[]{:S(2)}, u32[]{:S(2)}) async-start(bf16[8,64,128]{2,0,1:T(8,128)(2,1)} %bitcast.12), calls=%async_computation | async-start | bytes 262144 | tf_op jit(solution)/shard_map/all_to_all | solution.py:121
  54.3 234.0 %all-gather.5.cloned.1.call-start = ((), (), s32[]{:S(2)}) async-start(), calls=%async_computation.3 | async-start | bytes 3194880 | tf_op jit(solution)/shard_map/all_gather | solution.py:134
  238.3 1.9 copy-start.1
  239.3 1.9 copy-start.2
  240.2 1.9 copy-start.3
  241.2 1.9 copy-start.4
  242.1 1.9 copy-start.5
  243.1 1.9 copy-start.6
  245.9 47.1 %copy-start.7 = (f32[512,128]{0,1:T(8,128)S(1)}, f32[512,128]{0,1:T(8,128)}, u32[]{:S(2)}) copy-start(f32[512,128]{0,1:T(8,128)} %copy.123) | copy-start | bytes 786436
Sparse Core Ops, SparseCore 0:
  19.9 130.3 all-gather.2
  153.2 135.1 all-gather.4
where the time goes:
time: 420 us; the launch traced here: 419 us
  blocking collectives  139 us (33%)
  waiting for transfers between devices  136 us (32%)
  local copies, waits for them, and re-layouts  58.8 us (14%)
  matrix products  53 us (13%)
  starting transfers between devices  15.4 us (4%)
  between operations  13.6 us (3%)
    psum x1, blocking collectives, local(): scores = lax.psum(partial_scores, ('dp', 'owner'))  111 us
    all_gather x1, waiting for transfers between devices, local(): query_all = lax.all_gather(query_rot, 'dp', axis=0, tiled=True)  80.6 us
    all_gather x1, waiting for transfers between devices, local(): piece_slots = lax.all_gather(train_local, 'dp', axis=0, tiled=True)  42.4 us
    all_to_all x1, blocking collectives, local(): lax.all_to_all(train_in, 'dp', split_axis=1, concat_axis=0, tiled=True)  28.1 us
    dot_general x8, matrix products, condition(): jnp.einsum('fnb,ncb->fnc', damped.reshape(-1, in_blocks, in_width), basis...  24.3 us
    dot_general x8, matrix products, condition(): jnp.einsum('ckl,cld->ckd', basis_out, half_back.reshape(capacity, block_w...  18.7 us
    another operation x9, local copies, waits for them, and re-layouts, condition(): return jnp.stack(results)  16.5 us
    convert_element_type x8, local copies, waits for them, and re-layouts, condition(): restored = jnp.einsum('ckl,cld->ckd', basis_out, half_back.reshape(capaci...  15.3 us
  transfers between devices with their start and end apart: 4, of which 4 were waited for; matrix products, arithmetic and copies ran while one was open for 24% of the time, Pallas kernels for 0%

commit v1 on v0

v1 whole, which is shorter than its diff:
```python
import math

import jax
import jax.numpy as jnp
from jax import lax
from jax.experimental import pallas as pl
from jax.experimental.pallas import tpu as pltpu
from jax.sharding import Mesh, PartitionSpec as P


NQ = 8
ET = 16
DAMPING = 0.1
NZ, NY, NX, NC = 16, 4, 4, 2
BF = jnp.bfloat16
F32 = jnp.float32
INTERPRET = False


def swap_core(array):
    return lax.ppermute(array, "c", [(0, 1), (1, 0)])


def exchange(array, axis):
    return lax.all_to_all(array, axis, split_axis=0, concat_axis=0, tiled=True)


def prepare(owner_map, place, eigvals, basis_out):
    capacity, bk = basis_out.shape[0], basis_out.shape[1]
    ba = eigvals.shape[1]
    own_blocks = owner_map.shape[0] // (NX * NC)
    mine = own_blocks // NY

    def body(map_ref, place_ref, eig_ref, basis_ref, wk_ref, ws_ref, bk_ref, bs_ref, slot_ref, own_ref):
        x, y, c = place_ref[0], place_ref[1], place_ref[2]
        owner = NC * x + c
        count = jnp.int32(0)
        for p in range(NC * own_blocks):
            is_own = (map_ref[x * (NC * own_blocks) + p] == owner).astype(jnp.int32)
            slot_ref[p] = jnp.minimum(count, capacity - 1)
            own_ref[p] = is_own
            count = count + is_own
        for side, w_out, b_out in ((c, wk_ref, bk_ref), (1 - c, ws_ref, bs_ref)):
            for i in range(own_blocks):
                p = side * own_blocks + i
                start = pl.multiple_of(slot_ref[p] * bk, bk)
                values = 1.0 / (eig_ref[pl.ds(start, bk), :] + DAMPING)
                w_out[i] = jnp.where(own_ref[p] > 0, values, 0.0).astype(BF)
            for k in range(mine):
                p = side * own_blocks + mine * y + k
                block = basis_ref[slot_ref[p]].astype(F32)
                b_out[k] = jnp.where(own_ref[p] > 0, block, 0.0).astype(BF)

    w_shape = jax.ShapeDtypeStruct((own_blocks, bk, ba), BF)
    b_shape = jax.ShapeDtypeStruct((mine, bk, bk), BF)
    smem = pl.BlockSpec(memory_space=pltpu.SMEM)
    vmem = pl.BlockSpec(memory_space=pltpu.VMEM)
    return pl.pallas_call(
        body,
        out_shape=(w_shape, w_shape, b_shape, b_shape),
        in_specs=[smem, smem, vmem, vmem],
        out_specs=(vmem,) * 4,
        scratch_shapes=[pltpu.SMEM((NC * own_blocks,), jnp.int32)] * 2,
        name="prepare",
        interpret=INTERPRET,
    )(owner_map, place, eigvals, basis_out)


def score(place, most, rest, b_keep, b_recv, act, other, weights, scale):
    seg, fdim = rest.shape
    n_tok = NY * seg
    groups = most.shape[0] // seg
    mine, bk = b_keep.shape[0], b_keep.shape[1]
    ba = act.shape[-1]
    ddim = NY * ba
    per = seg // NQ
    half = NY // 2
    w_at = weights.shape[1] - fdim

    def body(place_ref, q_ref, t_ref, bk_ref, br_ref, a_ref, o_ref, w_ref, out_ref, qr, tr, qa, ta, dm, ex):
        first = place_ref[2] == 0
        for b in range(mine):
            cut = slice(bk * b, bk * b + bk)
            basis = (bk_ref[b].astype(F32) + br_ref[b].astype(F32)).astype(BF)
            tail = jnp.dot(t_ref[:, cut], basis, preferred_element_type=F32)
            turned = jnp.dot(q_ref[:, cut], basis, preferred_element_type=F32)
            turned = turned.reshape(NZ, groups, seg // NZ, bk)
            for g in range(groups + 1):
                block = (turned[:, g].reshape(seg, bk) if g < groups else tail).astype(BF)
                if g >= NY:
                    tr[seg * (g - NY) : seg * (g - NY + 1), cut] = block
                    continue
                for q in range(NQ):
                    at = NY * per * q + per * g
                    qr[at : at + per, cut] = block[per * q : per * q + per]

        def spread(q_from, t_from):
            for y in range(NY):
                for j in range(NY):
                    lanes = slice(ba * j, ba * j + ba)
                    ta[seg * y : seg * y + seg, lanes] = t_from[y, j]
                    for q in range(NQ):
                        at = NY * per * q + per * y
                        qa[at : at + per, lanes] = q_from[y, j, per * q : per * q + per]

        @pl.when(first)
        def _():
            spread(a_ref, o_ref)

        @pl.when(jnp.logical_not(first))
        def _():
            spread(o_ref, a_ref)

        for q in range(NQ):
            rows = slice(NY * per * q, NY * per * (q + 1))
            moment = lax.dot_general(
                qr[rows, :], qa[rows, :], (((0,), (0,)), ((), ())), preferred_element_type=F32
            )
            for j in range(NY):
                lanes = slice(ba * j, ba * j + ba)
                dm[q % 2, :, lanes] = (moment[:, lanes] * w_ref[j, w_at:, :].astype(F32)).astype(BF)
            proj = jnp.dot(tr[...], dm[q % 2], preferred_element_type=F32)
            total = jnp.zeros((n_tok, ba), F32)
            for j in range(NY):
                lanes = slice(ba * j, ba * j + ba)
                total = total + proj[:, lanes] * ta[:, lanes].astype(F32)
            parts = jnp.sum(total.reshape(half, 2, NZ, seg // NZ, ba), axis=(1, 3))
            for h in range(half):
                ex[q, pl.ds(h, NZ, stride=half), :] = parts[h]
        out_ref[...] = jnp.sum(ex[...], axis=2) * scale

    smem = pl.BlockSpec(memory_space=pltpu.SMEM)
    vmem = pl.BlockSpec(memory_space=pltpu.VMEM)
    return pl.pallas_call(
        body,
        out_shape=jax.ShapeDtypeStruct((NQ, half * NZ), F32),
        in_specs=[smem] + [vmem] * 7,
        out_specs=vmem,
        scratch_shapes=[
            pltpu.VMEM((n_tok, fdim), BF),
            pltpu.VMEM((n_tok, fdim), BF),
            pltpu.VMEM((n_tok, ddim), BF),
            pltpu.VMEM((n_tok, ddim), BF),
            pltpu.VMEM((2, fdim, ddim), BF),
            pltpu.VMEM((NQ, half * NZ, ba), F32),
        ],
        name="score",
        interpret=INTERPRET,
    )(place, most, rest, b_keep, b_recv, act, other, weights)


def local(query_out, query_in, train_out, train_in, basis_out, basis_in, eigvals, owner_map):
    x, y, c = lax.axis_index("x"), lax.axis_index("y"), lax.axis_index("c")
    ba = basis_in.shape[1]
    tok, units = query_out.shape
    width = query_in.shape[1]
    fdim = units // NY
    ddim = NY * ba
    ids = jnp.arange(4, dtype=jnp.int32)
    place = jnp.where(ids == 0, x, jnp.where(ids == 1, y, c)).astype(jnp.int32)

    both_out = jnp.concatenate([query_out, train_out], 0)
    rows = exchange(both_out.reshape(2 * tok, NY, fdim).transpose(1, 0, 2), "y")
    w_keep, w_send, b_keep, b_send = prepare(owner_map, place, eigvals, basis_out)
    q_rows = rows[:, :tok].reshape(NY * tok, fdim)
    t_rows = rows[:, tok:].reshape(NY * tok, fdim)
    n_ag = (NY - 1) * tok

    half_in = jnp.where(c == 0, query_in, train_in)
    cols = half_in.reshape(tok, NZ, ddim).transpose(1, 0, 2)
    last = jnp.broadcast_to(t_rows[None, n_ag:], (NZ, tok, fdim))
    mixed = exchange(jnp.concatenate([cols, last], 1), "z")
    w_own = (w_keep + swap_core(w_send)).reshape(NY, fdim, ba)
    b_recv = swap_core(b_send)
    most = jnp.concatenate([q_rows, t_rows[:n_ag]], 0)
    mixed, most, w_own, b_recv = lax.optimization_barrier((mixed, most, w_own, b_recv))
    rest = mixed[:, tok:].reshape(NZ * tok, fdim)

    in_cols = mixed[:, :tok].reshape(NZ * tok, NY, ba).transpose(1, 0, 2).reshape(NY * NZ * tok, ba)
    shared = jnp.concatenate([in_cols, basis_in[0]], 0)
    shared = jnp.broadcast_to(shared[None], (NY,) + shared.shape)
    packed = exchange(jnp.concatenate([shared, w_own], 1), "y")
    gathered = lax.all_gather(most, "z", axis=0, tiled=True)
    packed, gathered = lax.optimization_barrier((packed, gathered))

    n_in = NY * NZ * tok
    in_all = packed[:, :n_in].reshape(NY, NY, NZ * tok, ba)
    act = jnp.einsum("yjtb,jbc->yjtc", in_all, packed[:, n_in : n_in + ba], preferred_element_type=F32).astype(BF)
    other = swap_core(act)

    per = NZ * NY * tok // NQ
    hidden = units * NX * NC
    scale = 1.0 / math.sqrt(per * ET * hidden * width)
    scores = score(place, gathered, rest, b_keep, b_recv, act, other, packed, scale)

    flat = scores.reshape(1, -1, 128)
    flat = jnp.sum(exchange(jnp.broadcast_to(flat, (NY * NX * NC,) + flat.shape[1:]), ("y", "x", "c")), axis=0)[None]
    flat = jnp.sum(exchange(jnp.broadcast_to(flat, (NZ,) + flat.shape[1:]), "z"), axis=0)
    return flat.reshape(scores.shape)


def solution(mesh):
    fine = Mesh(mesh.devices.reshape(NZ, NY, NX, NC), ("z", "y", "x", "c"))
    dp, owner = ("z", "y"), ("x", "c")
    in_specs = (
        P(dp, owner),
        P(dp, None),
        P(dp, owner),
        P(dp, None),
        P(owner, None, None),
        P(dp, None, None),
        P(owner, dp),
        P(),
    )
    return jax.shard_map(local, mesh=fine, in_specs=in_specs, out_specs=P(), check_vma=False)
```

time: 420 us -> 134 us (0.32)
  waiting for transfers between devices: 136 us -> 7.12 us
  blocking collectives: 139 us -> 64.1 us
  local copies, waits for them, and re-layouts: 58.8 us -> 3.82 us
  matrix products: 53 us -> 0.29 us
  starting transfers between devices: 15.4 us -> 41.6 us
  between operations: 13.6 us -> 0.17 us
  Pallas kernels: 0 us -> 11.1 us
    all_gather x2 -> x0, waiting for transfers between devices: 123 us -> none  [the longest x1 80.6 us: local(): query_all = lax.all_gather(query_rot, 'dp', axis=0, tiled=True)]
    psum x1 -> x0, blocking collectives: 111 us -> none  [local(): scores = lax.psum(partial_scores, ('dp', 'owner'))]
    dot_general x23 -> x1, matrix products: 53 us -> 0.29 us  [local(): jnp.einsum('yjtb,jbc->yjtc', in_all, packed[:, n_in:n_in + ba], preferred...]
    all_gather x0 -> x1, blocking collectives: none -> 32 us  [local(): gathered = lax.all_gather(most, 'z', axis=0, tiled=True)]
    all_to_all x1 -> x3, starting transfers between devices: 6.4 us -> 23.4 us  [exchange(): return lax.all_to_all(array, axis, split_axis=0, concat_axis=0, tiled=True)]
    another operation x10 -> x0, local copies, waits for them, and re-layouts: 16.6 us -> none  [the longest x9 16.5 us: condition(): return jnp.stack(results)]
    convert_element_type x9 -> x0, local copies, waits for them, and re-layouts: 16.2 us -> none  [the longest x8 15.3 us: condition(): restored = jnp.einsum('ckl,cld->ckd', basis_out, half_back.reshape(capaci...]
    slice x10 -> x2, local copies, waits for them, and re-layouts: 11.4 us -> 0.04 us  [the longest x1 0.03 us: local(): in_all = packed[:, :n_in].reshape(NY, NY, NZ * tok, ba)]
  transfers between devices with their start and end apart: 4 -> 6, of which waited for: 4 -> 3; matrix products, arithmetic and copies ran while one was open for 24% -> 2% of each run, Pallas kernels for 0% -> 2%
where the time goes in v1:
time: 134 us
  blocking collectives  64.1 us (48%)
  starting transfers between devices  41.6 us (31%)
  Pallas kernels  11.1 us (8%)
  waiting for transfers between devices  7.12 us (5%)
  other arithmetic  5.36 us (4%)
  local copies, waits for them, and re-layouts  3.82 us (3%)
    all_to_all x2, blocking collectives, exchange(): return lax.all_to_all(array, axis, split_axis=0, concat_axis=0, tiled=True)  32.1 us
    all_gather x1, blocking collectives, local(): gathered = lax.all_gather(most, 'z', axis=0, tiled=True)  32 us
    all_to_all x3, starting transfers between devices, exchange(): return lax.all_to_all(array, axis, split_axis=0, concat_axis=0, tiled=True)  23.4 us
    ppermute x3, starting transfers between devices, swap_core(): return lax.ppermute(array, 'c', [(0, 1), (1, 0)])  18.1 us
    pallas_call x1, Pallas kernels, score(): pl.pallas_call(body, out_shape=jax.ShapeDtypeStruct((NQ, half * NZ), F32)...  7.83 us
    ppermute x3, waiting for transfers between devices, swap_core(): return lax.ppermute(array, 'c', [(0, 1), (1, 0)])  3.57 us
    all_to_all x3, waiting for transfers between devices, exchange(): return lax.all_to_all(array, axis, split_axis=0, concat_axis=0, tiled=True)  3.56 us
    pallas_call x1, Pallas kernels, prepare(): pl.pallas_call(body, out_shape=(w_shape, w_shape, b_shape, b_shape), in_s...  3.27 us
  transfers between devices with their start and end apart: 6, of which 3 were waited for; matrix products, arithmetic and copies ran while one was open for 2% of the time, Pallas kernels for 2%

profile of v1, /device:TPU:1, one launch (start us, length us, event | category | flops | bytes accessed | tf_op | source)
XLA Modules:
  0.0 133.6 jit_solution(14107969638243153405)
XLA Ops:
  0.0 0.8 pad_maximum_fusion.3
  0.8 0.6 copy.34
  1.4 5.0 %all-to-all-start = ((bf16[4,16,512]{2,1,0:T(8,128)(2,1)}), bf16[4,16,512]{2,1,0:T(8,128)(2,1)S(1)}, u32[]{:S(2)}, u32[]{:S(2)}) async-start(bf16[4,16,512]{2,1,0:T(8,128)(2,1)} %bitcast.29), calls=%async_computation | async-start | bytes 131072 | tf_op jit(solution)/shard_map/all_to_all | solution.py:25
  6.4 0.9 broadcast_select_fusion
  7.3 3.6 %all-to-all-done = bf16[4,16,512]{2,1,0:T(8,128)(2,1)S(1)} async-done(((bf16[4,16,512]{2,1,0:T(8,128)(2,1)}), bf16[4,16,512]{2,1,0:T(8,128)(2,1)S(1)}, u32[]{:S(2)}, u32[]{:S(2)}) %all-to-all-start) | async-done | bytes 65568 | tf_op jit(solution)/shard_map/all_to_all | solution.py:25
  10.9 0.7 pad_maximum_fusion.1
  11.6 14.9 %all-to-all-start.1 = ((bf16[16,16,512]{2,1,0:T(8,128)(2,1)}), bf16[16,16,512]{2,1,0:T(8,128)(2,1)S(1)}, u32[]{:S(2)}, u32[]{:S(2)}) async-start(bf16[16,16,512]{2,1,0:T(8,128)(2,1)} %pad_maximum_fusion.1), calls=%async_computation.1 | async-start | bytes 524288 | tf_op jit(solution)/shard_map/all_to_all | solution.py:25
  26.6 0.5 compare_select_fusion.1.place_ref
  27.1 3.3 %prepare.1 = (bf16[8,256,128]{2,1,0:T(8,128)(2,1)}, bf16[8,256,128]{2,1,0:T(8,128)(2,1)}, bf16[2,256,256]{2,1,0:T(8,128)(2,1)}, bf16[2,256,256]{2,1,0:T(8,128)(2,1)}) custom-call(s32[64]{0:T(128)} %map_ref.1, s32[4]{0:T(128)} %compare_select_fusion.1.place_ref, f32[3072,128]{1,0:T(8,128)} %eig_ref.1, bf16[12,256,256]{2,1,0:T(8,128)(2,1)} %basis_ref.1), custom_call_target="tpu_custom_call" | custom-call | tf_op jit(solution)/shard_map/prepare/pallas_call | solution.py:58
  30.4 4.3 %collective-permute-start.1 = (bf16[2,256,256]{2,1,0:T(8,128)(2,1)}, bf16[2,256,256]{2,1,0:T(8,128)(2,1)S(1)}, u32[]{:S(2)}, u32[]{:S(2)}) collective-permute-start(bf16[2,256,256]{2,1,0:T(8,128)(2,1)} %get-tuple-element.17), channel_id=1, source_target_pairs={{0,1},{1,0},{2,3},{3,2},{4,5},{5,4},{6,7},{7,6},{8,9},{9,8},{10,11... | collective-permute-start | bytes 786440 | tf_op jit(solution)/shard_map/ppermute | solution.py:21
  34.7 1.9 %collective-permute-start = (bf16[8,256,128]{2,1,0:T(8,128)(2,1)}, bf16[8,256,128]{2,1,0:T(8,128)(2,1)S(1)}, u32[]{:S(2)}, u32[]{:S(2)}) collective-permute-start(bf16[8,256,128]{2,1,0:T(8,128)(2,1)} %get-tuple-element.16), channel_id=1, source_target_pairs={{0,1},{1,0},{2,3},{3,2},{4,5},{5,4},{6,7},{7,6},{8,9},{9,8},{10,11... | collective-permute-start | bytes 1572872 | tf_op jit(solution)/shard_map/ppermute | solution.py:21
  36.6 2.0 %collective-permute-done = bf16[8,256,128]{2,1,0:T(8,128)(2,1)S(1)} collective-permute-done((bf16[8,256,128]{2,1,0:T(8,128)(2,1)}, bf16[8,256,128]{2,1,0:T(8,128)(2,1)S(1)}, u32[]{:S(2)}, u32[]{:S(2)}) %collective-permute-start) | collective-permute-done | bytes 524320 | tf_op jit(solution)/shard_map/ppermute | solution.py:21
  38.7 0.0 copy-start.4
  38.7 1.2 add.3
  39.9 0.0 collective-permute-done.1.br_ref
  39.9 0.0 copy-start.3
  39.9 0.0 all-to-all-done.1
  39.9 0.7 slice_bitcast_fusion
  40.7 0.0 copy-done.4
  40.7 0.1 broadcast_in_dim.44
  40.8 1.1 pad_maximum_fusion
  41.9 0.0 copy-done.3
  41.9 3.5 %all-to-all-start.2 = ((bf16[4,1152,128]{2,1,0:T(8,128)(2,1)}), bf16[4,1152,128]{2,1,0:T(8,128)(2,1)S(1)}, u32[]{:S(2)}, u32[]{:S(2)}) async-start(bf16[4,1152,128]{2,1,0:T(8,128)(2,1)} %pad_maximum_fusion), calls=%async_computation.2 | async-start | bytes 2359296 | tf_op jit(solution)/shard_map/all_to_all | solution.py:25
  45.5 32.0 %all_gather.3.q_ref = bf16[896,512]{1,0:T(8,128)(2,1)} all-gather(bf16[56,512]{1,0:T(8,128)(2,1)S(1)} %pad_maximum_fusion.4), channel_id=1, replica_groups=mesh['z'=16,'y'=4,'x'=4,'c'=2] {'z'}, dimensions={0}, use_global_device_ids=true | all-gather | bytes 974848 | tf_op jit(solution)/shard_map/all_gather | solution.py:183
  77.5 0.0 all-to-all-done.2.w_ref
  77.5 0.0 copy-start
  77.5 0.3 fusion.a_ref
  77.8 0.0 copy-start.1
  77.8 11.9 %collective-permute-start.2 = (bf16[4,4,128,128]{3,2,1,0:T(8,128)(2,1)S(1)}, bf16[4,4,128,128]{3,2,1,0:T(8,128)(2,1)S(1)}, u32[]{:S(2)}, u32[]{:S(2)}) collective-permute-start(bf16[4,4,128,128]{3,2,1,0:T(8,128)(2,1)S(1)} %fusion.a_ref), channel_id=1, source_target_pairs={{0,1},{1,0},{2,3},{3,2},{4,5},{5,4},{6,7},{7,6},{8,9},{9,8},{10,11... | collective-permute-start | bytes 1572872 | tf_op jit(solution)/shard_map/ppermute | solution.py:21
  89.8 1.5 %collective-permute-done.2.o_ref = bf16[4,4,128,128]{3,2,1,0:T(8,128)(2,1)S(1)} collective-permute-done((bf16[4,4,128,128]{3,2,1,0:T(8,128)(2,1)S(1)}, bf16[4,4,128,128]{3,2,1,0:T(8,128)(2,1)S(1)}, u32[]{:S(2)}, u32[]{:S(2)}) %collective-permute-start.2) | collective-permute-done | bytes 524320 | tf_op jit(solution)/shard_map/ppermute | solution.py:21
  91.3 0.0 copy-start.2
  91.3 0.0 copy-done
  91.3 0.0 copy-done.1
  91.3 0.8 copy-done.2
  92.1 7.8 %score.1 = f32[8,32]{1,0:T(8,128)} custom-call(s32[4]{0:T(128)} %compare_select_fusion.1.place_ref, bf16[896,512]{1,0:T(8,128)(2,1)} %all_gather.3.q_ref, bf16[128,512]{1,0:T(8,128)(2,1)} %get-tuple-element.25.t_ref, bf16[2,256,256]{2,1,0:T(8,128)(2,1)} %get-tuple-element.22.bk_ref, bf16[2,256,256]{2,1,0:T(8,128)(2,1)} %copy-done.3, ...), custom_call_target="tpu_custom_call" | custom-call | tf_op jit(solution)/shard_map/score/pallas_call | solution.py:134
  99.9 0.8 broadcast_in_dim.45
  100.7 14.8 %all_to_all.25 = f32[32,2,128]{2,1,0:T(2,128)S(1)} all-to-all(f32[32,2,128]{2,1,0:T(2,128)S(1)} %broadcast_in_dim.46), channel_id=1, replica_groups=mesh['z'=16,'y'=4,'x'=4,'c'=2] {'y','x','c'}, dimensions={0} | all-to-all | bytes 65536 | tf_op jit(solution)/shard_map/all_to_all | solution.py:25
  115.6 17.3 %all_to_all.26 = f32[16,2,128]{2,1,0:T(2,128)S(1)} all-to-all(f32[16,2,128]{2,1,0:T(2,128)S(1)} %broadcast_in_dim.47), channel_id=1, replica_groups=mesh['z'=16,'y'=4,'x'=4,'c'=2] {'z'}, dimensions={0} | all-to-all | bytes 32768 | tf_op jit(solution)/shard_map/all_to_all | solution.py:25
  132.9 0.7 reshape.43
  (13 shorter events, 0.2 us)
Async XLA Ops:
  1.4 9.5 %all-to-all-start = ((bf16[4,16,512]{2,1,0:T(8,128)(2,1)}), bf16[4,16,512]{2,1,0:T(8,128)(2,1)S(1)}, u32[]{:S(2)}, u32[]{:S(2)}) async-start(bf16[4,16,512]{2,1,0:T(8,128)(2,1)} %bitcast.29), calls=%async_computation | async-start | bytes 131072 | tf_op jit(solution)/shard_map/all_to_all | solution.py:25
  11.6 28.3 %all-to-all-start.1 = ((bf16[16,16,512]{2,1,0:T(8,128)(2,1)}), bf16[16,16,512]{2,1,0:T(8,128)(2,1)S(1)}, u32[]{:S(2)}, u32[]{:S(2)}) async-start(bf16[16,16,512]{2,1,0:T(8,128)(2,1)} %pad_maximum_fusion.1), calls=%async_computation.1 | async-start | bytes 524288 | tf_op jit(solution)/shard_map/all_to_all | solution.py:25
  30.4 9.5 %collective-permute-start.1 = (bf16[2,256,256]{2,1,0:T(8,128)(2,1)}, bf16[2,256,256]{2,1,0:T(8,128)(2,1)S(1)}, u32[]{:S(2)}, u32[]{:S(2)}) collective-permute-start(bf16[2,256,256]{2,1,0:T(8,128)(2,1)} %get-tuple-element.17), channel_id=1, source_target_pairs={{0,1},{1,0},{2,3},{3,2},{4,5},{5,4},{6,7},{7,6},{8,9},{9,8},{10,11... | collective-permute-start | bytes 786440 | tf_op jit(solution)/shard_map/ppermute | solution.py:21
  34.7 4.0 %collective-permute-start = (bf16[8,256,128]{2,1,0:T(8,128)(2,1)}, bf16[8,256,128]{2,1,0:T(8,128)(2,1)S(1)}, u32[]{:S(2)}, u32[]{:S(2)}) collective-permute-start(bf16[8,256,128]{2,1,0:T(8,128)(2,1)} %get-tuple-element.16), channel_id=1, source_target_pairs={{0,1},{1,0},{2,3},{3,2},{4,5},{5,4},{6,7},{7,6},{8,9},{9,8},{10,11... | collective-permute-start | bytes 1572872 | tf_op jit(solution)/shard_map/ppermute | solution.py:21
  38.7 2.0 %copy-start.4 = (bf16[1,128,128]{2,1,0:T(8,128)(2,1)S(1)}, bf16[1,128,128]{2,1,0:T(8,128)(2,1)}, u32[]{:S(2)}) copy-start(bf16[1,128,128]{2,1,0:T(8,128)(2,1)} %param.13) | copy-start | bytes 98308
  39.9 2.0 %copy-start.3 = (bf16[2,256,256]{2,1,0:T(8,128)(2,1)}, bf16[2,256,256]{2,1,0:T(8,128)(2,1)S(1)}, u32[]{:S(2)}) copy-start(bf16[2,256,256]{2,1,0:T(8,128)(2,1)S(1)} %collective-permute-done.1.br_ref) | copy-start | bytes 786436
  41.9 35.6 %all-to-all-start.2 = ((bf16[4,1152,128]{2,1,0:T(8,128)(2,1)}), bf16[4,1152,128]{2,1,0:T(8,128)(2,1)S(1)}, u32[]{:S(2)}, u32[]{:S(2)}) async-start(bf16[4,1152,128]{2,1,0:T(8,128)(2,1)} %pad_maximum_fusion), calls=%async_computation.2 | async-start | bytes 2359296 | tf_op jit(solution)/shard_map/all_to_all | solution.py:25
  77.5 13.8 %copy-start = (bf16[4,1152,128]{2,1,0:T(8,128)(2,1)}, bf16[4,1152,128]{2,1,0:T(8,128)(2,1)S(1)}, u32[]{:S(2)}) copy-start(bf16[4,1152,128]{2,1,0:T(8,128)(2,1)S(1)} %all-to-all-done.2.w_ref) | copy-start | bytes 3538948
  77.8 13.5 %copy-start.1 = (bf16[4,4,128,128]{3,2,1,0:T(8,128)(2,1)}, bf16[4,4,128,128]{3,2,1,0:T(8,128)(2,1)S(1)}, u32[]{:S(2)}) copy-start(bf16[4,4,128,128]{3,2,1,0:T(8,128)(2,1)S(1)} %fusion.a_ref) | copy-start | bytes 1572868
  77.8 13.5 %collective-permute-start.2 = (bf16[4,4,128,128]{3,2,1,0:T(8,128)(2,1)S(1)}, bf16[4,4,128,128]{3,2,1,0:T(8,128)(2,1)S(1)}, u32[]{:S(2)}, u32[]{:S(2)}) collective-permute-start(bf16[4,4,128,128]{3,2,1,0:T(8,128)(2,1)S(1)} %fusion.a_ref), channel_id=1, source_target_pairs={{0,1},{1,0},{2,3},{3,2},{4,5},{5,4},{6,7},{7,6},{8,9},{9,8},{10,11... | collective-permute-start | bytes 1572872 | tf_op jit(solution)/shard_map/ppermute | solution.py:21
  91.3 0.8 copy-start.2

commit v2 on v1

--- a/solution.py
+++ b/solution.py
@@ -62,28 +62,29 @@
         out_specs=(vmem,) * 4,
         scratch_shapes=[pltpu.SMEM((NC * own_blocks,), jnp.int32)] * 2,
         name="prepare",
+        compiler_params=pltpu.CompilerParams(vmem_limit_bytes=24 << 20),
         interpret=INTERPRET,
     )(owner_map, place, eigvals, basis_out)
 
 
-def score(place, most, rest, b_keep, b_recv, act, other, weights, scale):
+def score(most, rest, b_keep, b_recv, packed, scale):
     seg, fdim = rest.shape
     n_tok = NY * seg
     groups = most.shape[0] // seg
     mine, bk = b_keep.shape[0], b_keep.shape[1]
-    ba = act.shape[-1]
+    ba = packed.shape[-1]
     ddim = NY * ba
     per = seg // NQ
     half = NY // 2
-    w_at = weights.shape[1] - fdim
-
-    def body(place_ref, q_ref, t_ref, bk_ref, br_ref, a_ref, o_ref, w_ref, out_ref, qr, tr, qa, ta, dm, ex):
-        first = place_ref[2] == 0
+    basis_at = 2 * NY * seg
+    w_at = basis_at + ba
+
+    def body(m_ref, t_ref, bk_ref, br_ref, p_ref, out_ref, qr, tr, qa, ta, dm, ex):
         for b in range(mine):
             cut = slice(bk * b, bk * b + bk)
             basis = (bk_ref[b].astype(F32) + br_ref[b].astype(F32)).astype(BF)
             tail = jnp.dot(t_ref[:, cut], basis, preferred_element_type=F32)
-            turned = jnp.dot(q_ref[:, cut], basis, preferred_element_type=F32)
+            turned = jnp.dot(m_ref[:, cut], basis, preferred_element_type=F32)
             turned = turned.reshape(NZ, groups, seg // NZ, bk)
             for g in range(groups + 1):
                 block = (turned[:, g].reshape(seg, bk) if g < groups else tail).astype(BF)
@@ -93,24 +94,16 @@
                 for q in range(NQ):
                     at = NY * per * q + per * g
                     qr[at : at + per, cut] = block[per * q : per * q + per]
-
-        def spread(q_from, t_from):
+        for j in range(NY):
+            lanes = slice(ba * j, ba * j + ba)
+            basis = p_ref[j, basis_at:w_at, :]
             for y in range(NY):
-                for j in range(NY):
-                    lanes = slice(ba * j, ba * j + ba)
-                    ta[seg * y : seg * y + seg, lanes] = t_from[y, j]
-                    for q in range(NQ):
-                        at = NY * per * q + per * y
-                        qa[at : at + per, lanes] = q_from[y, j, per * q : per * q + per]
-
-        @pl.when(first)
-        def _():
-            spread(a_ref, o_ref)
-
-        @pl.when(jnp.logical_not(first))
-        def _():
-            spread(o_ref, a_ref)
-
+                raw = p_ref[y, 2 * seg * j : 2 * seg * (j + 1), :]
+                block = jnp.dot(raw, basis, preferred_element_type=F32).astype(BF)
+                ta[seg * y : seg * y + seg, lanes] = block[seg:]
+                for q in range(NQ):
+                    at = NY * per * q + per * y
+                    qa[at : at + per, lanes] = block[per * q : per * q + per]
         for q in range(NQ):
             rows = slice(NY * per * q, NY * per * (q + 1))
             moment = lax.dot_general(
@@ -118,7 +111,7 @@
             )
             for j in range(NY):
                 lanes = slice(ba * j, ba * j + ba)
-                dm[q % 2, :, lanes] = (moment[:, lanes] * w_ref[j, w_at:, :].astype(F32)).astype(BF)
+                dm[q % 2, :, lanes] = (moment[:, lanes] * p_ref[j, w_at:, :].astype(F32)).astype(BF)
             proj = jnp.dot(tr[...], dm[q % 2], preferred_element_type=F32)
             total = jnp.zeros((n_tok, ba), F32)
             for j in range(NY):
@@ -127,14 +120,13 @@
             parts = jnp.sum(total.reshape(half, 2, NZ, seg // NZ, ba), axis=(1, 3))
             for h in range(half):
                 ex[q, pl.ds(h, NZ, stride=half), :] = parts[h]
-        out_ref[...] = jnp.sum(ex[...], axis=2) * scale
-
-    smem = pl.BlockSpec(memory_space=pltpu.SMEM)
+        out_ref[...] = jnp.sum(ex[:, : half * NZ, :], axis=2) * scale
+
     vmem = pl.BlockSpec(memory_space=pltpu.VMEM)
     return pl.pallas_call(
         body,
-        out_shape=jax.ShapeDtypeStruct((NQ, half * NZ), F32),
-        in_specs=[smem] + [vmem] * 7,
+        out_shape=pltpu.VMEM((NQ, half * NZ), F32),
+        in_specs=[vmem] * 5,
         out_specs=vmem,
         scratch_shapes=[
             pltpu.VMEM((n_tok, fdim), BF),
@@ -142,11 +134,12 @@
             pltpu.VMEM((n_tok, ddim), BF),
             pltpu.VMEM((n_tok, ddim), BF),
             pltpu.VMEM((2, fdim, ddim), BF),
-            pltpu.VMEM((NQ, half * NZ, ba), F32),
+            pltpu.VMEM((NQ, half * NZ + 8, ba), F32),
         ],
         name="score",
+        compiler_params=pltpu.CompilerParams(vmem_limit_bytes=24 << 20),
         interpret=INTERPRET,
-    )(place, most, rest, b_keep, b_recv, act, other, weights)
+    )(most, rest, b_keep, b_recv, packed)
 
 
 def local(query_out, query_in, train_out, train_in, basis_out, basis_in, eigvals, owner_map):
@@ -176,22 +169,19 @@
     mixed, most, w_own, b_recv = lax.optimization_barrier((mixed, most, w_own, b_recv))
     rest = mixed[:, tok:].reshape(NZ * tok, fdim)
 
-    in_cols = mixed[:, :tok].reshape(NZ * tok, NY, ba).transpose(1, 0, 2).reshape(NY * NZ * tok, ba)
-    shared = jnp.concatenate([in_cols, basis_in[0]], 0)
+    in_cols = mixed[:, :tok].reshape(NZ * tok, NY, ba).transpose(1, 0, 2)
+    other = swap_core(in_cols)
+    pair = jnp.stack([jnp.where(c == 0, in_cols, other), jnp.where(c == 0, other, in_cols)], 1)
+    shared = jnp.concatenate([pair.reshape(-1, ba), basis_in[0]], 0)
     shared = jnp.broadcast_to(shared[None], (NY,) + shared.shape)
     packed = exchange(jnp.concatenate([shared, w_own], 1), "y")
     gathered = lax.all_gather(most, "z", axis=0, tiled=True)
     packed, gathered = lax.optimization_barrier((packed, gathered))
 
-    n_in = NY * NZ * tok
-    in_all = packed[:, :n_in].reshape(NY, NY, NZ * tok, ba)
-    act = jnp.einsum("yjtb,jbc->yjtc", in_all, packed[:, n_in : n_in + ba], preferred_element_type=F32).astype(BF)
-    other = swap_core(act)
-
     per = NZ * NY * tok // NQ
     hidden = units * NX * NC
     scale = 1.0 / math.sqrt(per * ET * hidden * width)
-    scores = score(place, gathered, rest, b_keep, b_recv, act, other, packed, scale)
+    scores = score(gathered, rest, b_keep, b_recv, packed, scale)
 
     flat = scores.reshape(1, -1, 128)
     flat = jnp.sum(exchange(jnp.broadcast_to(flat, (NY * NX * NC,) + flat.shape[1:]), ("y", "x", "c")), axis=0)[None]

time: 134 us -> 126 us (0.940)
  Pallas kernels: 11.1 us -> 6.24 us
  starting transfers between devices: 41.6 us -> 38.5 us
    all_to_all x2, blocking collectives: 32.1 us -> 36.3 us  [exchange(): return lax.all_to_all(array, axis, split_axis=0, concat_axis=0, tiled=True)]
    all_gather x1, blocking collectives: 32 us -> 28.8 us  [local(): gathered = lax.all_gather(most, 'z', axis=0, tiled=True)]
    ppermute x3, starting transfers between devices: 18.1 us -> 15.1 us  [swap_core(): return lax.ppermute(array, 'c', [(0, 1), (1, 0)])]
    pallas_call x1, Pallas kernels: 7.83 us -> 5.28 us  [score(): pl.pallas_call(body, out_shape=pltpu.VMEM((NQ, half * NZ), F32), in_specs...]
    pallas_call x1, Pallas kernels: 3.27 us -> 0.96 us  [prepare(): pl.pallas_call(body, out_shape=(w_shape, w_shape, b_shape, b_shape), in_s...]
    all_to_all x3, waiting for transfers between devices: 3.56 us -> 5.6 us  [exchange(): return lax.all_to_all(array, axis, split_axis=0, concat_axis=0, tiled=True)]
  transfers between devices with their start and end apart: 6 -> 6, of which waited for: 3 -> 4; matrix products, arithmetic and copies ran while one was open for 2% -> 1% of each run, Pallas kernels for 2% -> 1%
where the time goes in v2:
time: 126 us
  blocking collectives  65.1 us (52%)
  starting transfers between devices  38.5 us (31%)
  waiting for transfers between devices  8.41 us (7%)
  Pallas kernels  6.24 us (5%)
  other arithmetic  4.18 us (3%)
  local copies, waits for them, and re-layouts  3.07 us (2%)
    all_to_all x2, blocking collectives, exchange(): return lax.all_to_all(array, axis, split_axis=0, concat_axis=0, tiled=True)  36.3 us
    all_gather x1, blocking collectives, local(): gathered = lax.all_gather(most, 'z', axis=0, tiled=True)  28.8 us
    all_to_all x3, starting transfers between devices, exchange(): return lax.all_to_all(array, axis, split_axis=0, concat_axis=0, tiled=True)  23.5 us
    ppermute x3, starting transfers between devices, swap_core(): return lax.ppermute(array, 'c', [(0, 1), (1, 0)])  15.1 us
    all_to_all x3, waiting for transfers between devices, exchange(): return lax.all_to_all(array, axis, split_axis=0, concat_axis=0, tiled=True)  5.6 us
    pallas_call x1, Pallas kernels, score(): pl.pallas_call(body, out_shape=pltpu.VMEM((NQ, half * NZ), F32), in_specs...  5.28 us
    ppermute x3, waiting for transfers between devices, swap_core(): return lax.ppermute(array, 'c', [(0, 1), (1, 0)])  2.8 us
  transfers between devices with their start and end apart: 6, of which 4 were waited for; matrix products, arithmetic and copies ran while one was open for 1% of the time, Pallas kernels for 1%

profile of v2, /device:TPU:1, one launch (start us, length us, event | category | flops | bytes accessed | tf_op | source)
XLA Modules:
  0.0 125.8 jit_solution(4280256347813609928)
XLA Ops:
  0.0 0.0 copy-start.2
  0.0 0.0 copy-start
  0.0 0.9 pad_maximum_fusion.4
  0.9 0.6 copy.30
  1.5 5.0 %all-to-all-start = ((bf16[4,16,512]{2,1,0:T(8,128)(2,1)}), bf16[4,16,512]{2,1,0:T(8,128)(2,1)S(1)}, u32[]{:S(2)}, u32[]{:S(2)}) async-start(bf16[4,16,512]{2,1,0:T(8,128)(2,1)} %bitcast.33), calls=%async_computation | async-start | bytes 131072 | tf_op jit(solution)/shard_map/all_to_all | solution.py:25
  6.5 0.9 broadcast_select_fusion
  7.5 3.6 %all-to-all-done = bf16[4,16,512]{2,1,0:T(8,128)(2,1)S(1)} async-done(((bf16[4,16,512]{2,1,0:T(8,128)(2,1)}), bf16[4,16,512]{2,1,0:T(8,128)(2,1)S(1)}, u32[]{:S(2)}, u32[]{:S(2)}) %all-to-all-start) | async-done | bytes 65568 | tf_op jit(solution)/shard_map/all_to_all | solution.py:25
  11.0 0.7 pad_maximum_fusion.2
  11.8 14.9 %all-to-all-start.1 = ((bf16[16,16,512]{2,1,0:T(8,128)(2,1)}), bf16[16,16,512]{2,1,0:T(8,128)(2,1)S(1)}, u32[]{:S(2)}, u32[]{:S(2)}) async-start(bf16[16,16,512]{2,1,0:T(8,128)(2,1)} %pad_maximum_fusion.2), calls=%async_computation.1 | async-start | bytes 524288 | tf_op jit(solution)/shard_map/all_to_all | solution.py:25
  26.7 0.0 copy-done.2
  26.7 0.0 copy-done
  26.7 0.0 copy-start.1
  26.7 1.4 %copy-done.1 = bf16[12,256,256]{2,1,0:T(8,128)(2,1)S(1)} copy-done((bf16[12,256,256]{2,1,0:T(8,128)(2,1)S(1)}, bf16[12,256,256]{2,1,0:T(8,128)(2,1)}, u32[]{:S(2)}) %copy-start.1) | copy-done | bytes 1572888
  28.1 1.0 prepare.1
  29.1 4.3 %collective-permute-start.1 = (bf16[2,256,256]{2,1,0:T(8,128)(2,1)S(1)}, bf16[2,256,256]{2,1,0:T(8,128)(2,1)S(1)}, u32[]{:S(2)}, u32[]{:S(2)}) collective-permute-start(bf16[2,256,256]{2,1,0:T(8,128)(2,1)S(1)} %get-tuple-element.17), channel_id=1, source_target_pairs={{0,1},{1,0},{2,3},{3,2},{4,5},{5,4},{6,7},{7,6},{8,9},{9,8},{10,11... | collective-permute-start | bytes 786440 | tf_op jit(solution)/shard_map/ppermute | solution.py:21
  33.4 1.9 %collective-permute-start = (bf16[8,256,128]{2,1,0:T(8,128)(2,1)S(1)}, bf16[8,256,128]{2,1,0:T(8,128)(2,1)S(1)}, u32[]{:S(2)}, u32[]{:S(2)}) collective-permute-start(bf16[8,256,128]{2,1,0:T(8,128)(2,1)S(1)} %get-tuple-element.16), channel_id=1, source_target_pairs={{0,1},{1,0},{2,3},{3,2},{4,5},{5,4},{6,7},{7,6},{8,9},{9,8},{10,11... | collective-permute-start | bytes 1572872 | tf_op jit(solution)/shard_map/ppermute | solution.py:21
  35.4 1.8 %collective-permute-done = bf16[8,256,128]{2,1,0:T(8,128)(2,1)S(1)} collective-permute-done((bf16[8,256,128]{2,1,0:T(8,128)(2,1)S(1)}, bf16[8,256,128]{2,1,0:T(8,128)(2,1)S(1)}, u32[]{:S(2)}, u32[]{:S(2)}) %collective-permute-start) | collective-permute-done | bytes 524320 | tf_op jit(solution)/shard_map/ppermute | solution.py:21
  37.2 0.0 copy-start.3
  37.2 0.1 add.3
  37.4 0.0 collective-permute-done.1.br_ref
  37.4 2.0 %all-to-all-done.1 = bf16[16,16,512]{2,1,0:T(8,128)(2,1)S(1)} async-done(((bf16[16,16,512]{2,1,0:T(8,128)(2,1)}), bf16[16,16,512]{2,1,0:T(8,128)(2,1)S(1)}, u32[]{:S(2)}, u32[]{:S(2)}) %all-to-all-start.1) | async-done | bytes 262176 | tf_op jit(solution)/shard_map/all_to_all | solution.py:25
  39.5 8.8 %collective-permute-start.2 = (bf16[4,128,128]{2,1,0:T(8,128)(2,1)S(1)}, bf16[4,128,128]{2,1,0:T(8,128)(2,1)S(1)}, u32[]{:S(2)}, u32[]{:S(2)}) collective-permute-start(bf16[4,128,128]{2,1,0:T(8,128)(2,1)S(1)} %bitcast.38), channel_id=1, source_target_pairs={{0,1},{1,0},{2,3},{3,2},{4,5},{5,4},{6,7},{7,6},{8,9},{9,8},{10,11... | collective-permute-start | bytes 393224 | tf_op jit(solution)/shard_map/ppermute | solution.py:21
  48.4 1.0 collective-permute-done.2
  49.4 0.0 copy-done.3
  49.4 0.2 broadcast_in_dim.44
  49.6 1.3 %pad_maximum_fusion = bf16[4,1664,128]{2,1,0:T(8,128)(2,1)} fusion(bf16[4,512,128]{2,1,0:T(8,128)(2,1)S(1)} %bitcast.34, bf16[4,1152,128]{2,1,0:T(8,128)(2,1)S(1)} %broadcast_in_dim.44), kind=kLoop, calls=%fused_computation | loop fusion | flops 3407872 | bytes 3407872 | tf_op jit(solution)/shard_map/concatenate | solution.py:177
  50.9 3.6 %all-to-all-start.2 = ((bf16[4,1664,128]{2,1,0:T(8,128)(2,1)}), bf16[4,1664,128]{2,1,0:T(8,128)(2,1)S(1)}, u32[]{:S(2)}, u32[]{:S(2)}) async-start(bf16[4,1664,128]{2,1,0:T(8,128)(2,1)} %pad_maximum_fusion), calls=%async_computation.2 | async-start | bytes 3407872 | tf_op jit(solution)/shard_map/all_to_all | solution.py:25
  54.5 28.8 %all_gather.3.m_ref = bf16[896,512]{1,0:T(8,128)(2,1)S(1)} all-gather(bf16[56,512]{1,0:T(8,128)(2,1)S(1)} %pad_maximum_fusion.5), channel_id=1, replica_groups=mesh['z'=16,'y'=4,'x'=4,'c'=2] {'z'}, dimensions={0}, use_global_device_ids=true | all-gather | bytes 974848 | tf_op jit(solution)/shard_map/all_gather | solution.py:178
  83.3 0.0 all-to-all-done.2.p_ref
  83.3 5.3 %score.1 = f32[8,32]{1,0:T(8,128)S(1)} custom-call(bf16[896,512]{1,0:T(8,128)(2,1)S(1)} %all_gather.3.m_ref, bf16[128,512]{1,0:T(8,128)(2,1)S(1)} %get-tuple-element.25.t_ref, bf16[2,256,256]{2,1,0:T(8,128)(2,1)S(1)} %get-tuple-element.22.bk_ref, bf16[2,256,256]{2,1,0:T(8,128)(2,1)S(1)} %collective-permute-done.1.br_ref, ...), custom_call_target="tpu_custom_call" | custom-call | tf_op jit(solution)/shard_map/score/pallas_call | solution.py:126
  88.6 0.1 broadcast_in_dim.45
  88.7 19.6 %all_to_all.25 = f32[32,2,128]{2,1,0:T(2,128)S(1)} all-to-all(f32[32,2,128]{2,1,0:T(2,128)S(1)} %broadcast_in_dim.46), channel_id=1, replica_groups=mesh['z'=16,'y'=4,'x'=4,'c'=2] {'y','x','c'}, dimensions={0} | all-to-all | bytes 65536 | tf_op jit(solution)/shard_map/all_to_all | solution.py:25
  108.3 16.7 %all_to_all.26 = f32[16,2,128]{2,1,0:T(2,128)S(1)} all-to-all(f32[16,2,128]{2,1,0:T(2,128)S(1)} %broadcast_in_dim.47), channel_id=1, replica_groups=mesh['z'=16,'y'=4,'x'=4,'c'=2] {'z'}, dimensions={0} | all-to-all | bytes 32768 | tf_op jit(solution)/shard_map/all_to_all | solution.py:25
  125.1 0.7 reshape.39
  (16 shorter events, 0.3 us)
Async XLA Ops:
  0.0 26.7 %copy-start.2 = (s32[64]{0:T(128)S(1)}, s32[64]{0:T(128)}, u32[]{:S(2)}) copy-start(s32[64]{0:T(128)} %map_ref.1) | copy-start | bytes 772
  0.0 26.7 %copy-start = (f32[3072,128]{1,0:T(8,128)S(1)}, f32[3072,128]{1,0:T(8,128)}, u32[]{:S(2)}) copy-start(f32[3072,128]{1,0:T(8,128)} %eig_ref.1) | copy-start | bytes 4718596
  1.5 9.5 %all-to-all-start = ((bf16[4,16,512]{2,1,0:T(8,128)(2,1)}), bf16[4,16,512]{2,1,0:T(8,128)(2,1)S(1)}, u32[]{:S(2)}, u32[]{:S(2)}) async-start(bf16[4,16,512]{2,1,0:T(8,128)(2,1)} %bitcast.33), calls=%async_computation | async-start | bytes 131072 | tf_op jit(solution)/shard_map/all_to_all | solution.py:25
  11.8 27.6 %all-to-all-start.1 = ((bf16[16,16,512]{2,1,0:T(8,128)(2,1)}), bf16[16,16,512]{2,1,0:T(8,128)(2,1)S(1)}, u32[]{:S(2)}, u32[]{:S(2)}) async-start(bf16[16,16,512]{2,1,0:T(8,128)(2,1)} %pad_maximum_fusion.2), calls=%async_computation.1 | async-start | bytes 524288 | tf_op jit(solution)/shard_map/all_to_all | solution.py:25
  26.7 1.4 %copy-start.1 = (bf16[12,256,256]{2,1,0:T(8,128)(2,1)S(1)}, bf16[12,256,256]{2,1,0:T(8,128)(2,1)}, u32[]{:S(2)}) copy-start(bf16[12,256,256]{2,1,0:T(8,128)(2,1)} %basis_ref.1) | copy-start | bytes 4718596
  29.1 8.3 %collective-permute-start.1 = (bf16[2,256,256]{2,1,0:T(8,128)(2,1)S(1)}, bf16[2,256,256]{2,1,0:T(8,128)(2,1)S(1)}, u32[]{:S(2)}, u32[]{:S(2)}) collective-permute-start(bf16[2,256,256]{2,1,0:T(8,128)(2,1)S(1)} %get-tuple-element.17), channel_id=1, source_target_pairs={{0,1},{1,0},{2,3},{3,2},{4,5},{5,4},{6,7},{7,6},{8,9},{9,8},{10,11... | collective-permute-start | bytes 786440 | tf_op jit(solution)/shard_map/ppermute | solution.py:21
  33.4 3.8 %collective-permute-start = (bf16[8,256,128]{2,1,0:T(8,128)(2,1)S(1)}, bf16[8,256,128]{2,1,0:T(8,128)(2,1)S(1)}, u32[]{:S(2)}, u32[]{:S(2)}) collective-permute-start(bf16[8,256,128]{2,1,0:T(8,128)(2,1)S(1)} %get-tuple-element.16), channel_id=1, source_target_pairs={{0,1},{1,0},{2,3},{3,2},{4,5},{5,4},{6,7},{7,6},{8,9},{9,8},{10,11... | collective-permute-start | bytes 1572872 | tf_op jit(solution)/shard_map/ppermute | solution.py:21
  37.2 12.2 %copy-start.3 = (bf16[1,128,128]{2,1,0:T(8,128)(2,1)S(1)}, bf16[1,128,128]{2,1,0:T(8,128)(2,1)}, u32[]{:S(2)}) copy-start(bf16[1,128,128]{2,1,0:T(8,128)(2,1)} %param.13) | copy-start | bytes 98308
  39.5 9.8 %collective-permute-start.2 = (bf16[4,128,128]{2,1,0:T(8,128)(2,1)S(1)}, bf16[4,128,128]{2,1,0:T(8,128)(2,1)S(1)}, u32[]{:S(2)}, u32[]{:S(2)}) collective-permute-start(bf16[4,128,128]{2,1,0:T(8,128)(2,1)S(1)} %bitcast.38), channel_id=1, source_target_pairs={{0,1},{1,0},{2,3},{3,2},{4,5},{5,4},{6,7},{7,6},{8,9},{9,8},{10,11... | collective-permute-start | bytes 393224 | tf_op jit(solution)/shard_map/ppermute | solution.py:21
  50.9 32.4 %all-to-all-start.2 = ((bf16[4,1664,128]{2,1,0:T(8,128)(2,1)}), bf16[4,1664,128]{2,1,0:T(8,128)(2,1)S(1)}, u32[]{:S(2)}, u32[]{:S(2)}) async-start(bf16[4,1664,128]{2,1,0:T(8,128)(2,1)} %pad_maximum_fusion), calls=%async_computation.2 | async-start | bytes 3407872 | tf_op jit(solution)/shard_map/all_to_all | solution.py:25
